TPU v7x, 32 devices: a whole 2x2x4 slice. The times are simulated.
32 devices in a mesh: groups: 2 (over y), ctx: 4 (over z), tensor: 2 (over x), dp: 2 (over core).
Axes of the slice: x: 2, y: 2, z: 4, core: 2. Of those that a mesh axis runs over, the one named last changes fastest.
Arguments:
- tokens: bfloat16 [4, 1024, 1024], P(('groups', 'dp'), 'ctx', 'tensor'), parts along dimension 0
- w_qkv: bfloat16 [1024, 3, 1024], P(None, None, 'tensor')
- w_out: bfloat16 [1024, 1024], P('tensor'), may hold values from -0.1875 to 0.1875
- labels: int32 [4, 8, 1024], P(('groups', 'dp'), 'tensor', 'ctx'), parts along dimension 0, may hold values from 0 to 255, as said below
- grad_out: bfloat16 [4, 1024, 1024], P(('groups', 'dp'), 'ctx', 'tensor'), parts along dimension 0, may hold values from -6 to 6
Outputs:
- attended: bfloat16 [4, 1024, 1024], P(('groups', 'dp'), 'ctx', 'tensor'), parts along dimension 0
- grad_tokens: bfloat16 [4, 1024, 1024], P(('groups', 'dp'), 'ctx', 'tensor'), parts along dimension 0
- grad_w_qkv: float32 [2048, 3, 1024], P('groups', None, 'tensor'), parts along dimension 0
- grad_w_out: float32 [2048, 1024], P(('groups', 'tensor')), parts along dimension 0
There are 2 independent parts, one for each index of `groups`. A program takes and returns all parts, laid end to end along the dimension named above; an argument that names none is the same for every part. Nothing has to cross between parts.
Inputs may be any that keep to these rules, and one draw needn't show every extreme that they name: `labels`: cluster c of any head belongs to owner c % 4. Among the 256 tokens of one document on one index of ctx, at most 192 have, for one head, clusters of one owner; for each head one owner has exactly 192 from every such block, and the other owners share the rest of a block evenly (counts differ by at most one).
All inputs are finite; a program needn't handle non-finite values.
Results may differ from a plain program's by a relative error of at most 0.035.
The roundings to bfloat16 on the way count: a program that leaves them out, or rounds other values in their place, can miss the bound.
Values may be sent and summed in bfloat16 or wider, within the bound.
A program may use at most 64 MiB of HBM per device.

v0:
```python
import math
import jax
import jax.numpy as jnp
from jax import lax
from jax.sharding import PartitionSpec as P

HD = 128


def contract_last(left, right):
    return lax.dot_general(
        left, right, (((1,), (1,)), ((), ())), preferred_element_type=jnp.float32
    )


def contract_first(left, right):
    return lax.dot_general(
        left, right, (((0,), (0,)), ((), ())), preferred_element_type=jnp.float32
    )


def masked_probs(query_block, label_block, keys_in, marks):
    scores = contract_last(query_block, keys_in) * HD ** (-0.5)
    same = label_block[:, None] == marks[None, :]
    scores = jnp.where(same, scores, jnp.float32(-1e30))
    top_value = jnp.max(scores, axis=1, keepdims=True)
    expo = jnp.exp(scores - top_value)
    return expo / jnp.sum(expo, axis=1, keepdims=True)


def owner_forward(queries, keys_in, values_in, marks):
    total = queries.shape[0]
    block_rows = math.gcd(total, 512)
    block_count = total // block_rows

    def forward_block(index):
        start = index * block_rows
        query_block = lax.dynamic_slice_in_dim(queries, start, block_rows, 0)
        label_block = lax.dynamic_slice_in_dim(marks, start, block_rows, 0)
        probs = masked_probs(query_block, label_block, keys_in, marks).astype(jnp.bfloat16)
        return jnp.dot(probs, values_in, preferred_element_type=jnp.float32).astype(jnp.bfloat16)

    return lax.map(forward_block, jnp.arange(block_count, dtype=jnp.int32)).reshape(
        total, queries.shape[1]
    )


def owner_backward(queries, keys_in, values_in, marks, attention, cotangent):
    total, size = queries.shape
    block_rows = math.gcd(total, 512)
    block_count = total // block_rows

    def backward_block(carry, index):
        grad_keys, grad_values = carry
        start = index * block_rows
        query_block = lax.dynamic_slice_in_dim(queries, start, block_rows, 0)
        label_block = lax.dynamic_slice_in_dim(marks, start, block_rows, 0)
        attn_block = lax.dynamic_slice_in_dim(attention, start, block_rows, 0)
        cot_block = lax.dynamic_slice_in_dim(cotangent, start, block_rows, 0)
        probs_full = masked_probs(query_block, label_block, keys_in, marks)
        probs = probs_full.astype(jnp.bfloat16)
        dprob = contract_last(cot_block, values_in)
        delta = jnp.sum(
            cot_block.astype(jnp.float32) * attn_block.astype(jnp.float32), axis=1, keepdims=True
        )
        dscore = (probs_full * (dprob - delta) * HD ** (-0.5)).astype(jnp.bfloat16)
        grad_query = jnp.dot(dscore, keys_in, preferred_element_type=jnp.float32).astype(
            jnp.bfloat16
        )
        grad_keys = grad_keys + contract_first(dscore, query_block)
        grad_values = grad_values + contract_first(probs, cot_block)
        return ((grad_keys, grad_values), grad_query)

    empty = jnp.zeros((total, size), jnp.float32)
    (grad_keys, grad_values), grad_queries = lax.scan(
        backward_block, (empty, empty), jnp.arange(block_count, dtype=jnp.int32)
    )
    return (
        grad_queries.reshape(total, size),
        grad_keys.astype(jnp.bfloat16),
        grad_values.astype(jnp.bfloat16),
    )


def shards(tokens, w_qkv, w_out, labels, grad_out):
    rows_all, grads_all = (
        lax.all_gather(tokens, "tensor", axis=2, tiled=True),
        lax.all_gather(grad_out, "tensor", axis=2, tiled=True),
    )
    tok_rows = rows_all[0]
    tok_grads = grads_all[0]
    tok_count, width = tok_rows.shape
    heads_local = w_out.shape[0] // HD
    ctx_count = lax.axis_size("ctx")
    capacity = 3 * tok_count // ctx_count
    slot_total = ctx_count * capacity
    qkv = jnp.dot(
        tok_rows, w_qkv.reshape(width, 3 * heads_local * HD), preferred_element_type=jnp.float32
    )
    qkv = qkv.astype(jnp.bfloat16).reshape(tok_count, 3, heads_local, HD)
    qkv_heads = jnp.transpose(qkv, (2, 0, 1, 3)).reshape(heads_local, tok_count, 3 * HD)
    cotangent = contract_last(tok_grads, w_out).astype(jnp.bfloat16)
    cot_heads = jnp.transpose(cotangent.reshape(tok_count, heads_local, HD), (1, 0, 2))
    labels_local = labels[0]
    owner_of = labels_local % ctx_count
    owner_hits = (
        owner_of[:, :, None] == jnp.arange(ctx_count, dtype=jnp.int32)[None, None, :]
    ).astype(jnp.int32)
    earlier = jnp.cumsum(owner_hits, axis=1) - owner_hits
    slot_index = jnp.sum(earlier * owner_hits, axis=2)
    destination = owner_of * capacity + slot_index

    def pack(values):
        feature_count = values.shape[2]
        empty_buffer = jnp.zeros((heads_local, slot_total, feature_count), values.dtype)
        filled = jax.vmap(lambda buffer, where_to, rows_in: buffer.at[where_to].set(rows_in))(
            empty_buffer, destination, values
        )
        return filled.reshape(heads_local, ctx_count, capacity, feature_count)

    def unpack(received):
        flat = received.reshape(heads_local, slot_total, received.shape[3])
        return jax.vmap(lambda table, where_to: jnp.take(table, where_to, axis=0))(
            flat, destination
        )

    label_slots = jax.vmap(
        lambda where_to, marks: jnp.full((slot_total,), -1.0, jnp.bfloat16).at[where_to].set(marks)
    )(destination, labels_local.astype(jnp.bfloat16)).reshape(heads_local, ctx_count, capacity)
    arrived, arrived_marks = (
        lax.all_to_all(pack(qkv_heads), "ctx", split_axis=1, concat_axis=1, tiled=True),
        lax.all_to_all(label_slots, "ctx", split_axis=1, concat_axis=1, tiled=True),
    )
    arrived = arrived.reshape(heads_local, slot_total, 3 * HD)
    marks_own = arrived_marks.reshape(heads_local, slot_total)
    queries_own = arrived[:, :, :HD]
    keys_own = arrived[:, :, HD : 2 * HD]
    values_own = arrived[:, :, 2 * HD :]
    attention_own = jax.vmap(owner_forward)(queries_own, keys_own, values_own, marks_own)
    returned = lax.all_to_all(
        attention_own.reshape(heads_local, ctx_count, capacity, HD),
        "ctx",
        split_axis=1,
        concat_axis=1,
        tiled=True,
    )
    attention_tok = unpack(returned)
    cot_arrived = lax.all_to_all(pack(cot_heads), "ctx", split_axis=1, concat_axis=1, tiled=True)
    cot_own = cot_arrived.reshape(heads_local, slot_total, HD)
    grad_q, grad_k, grad_v = jax.vmap(owner_backward)(
        queries_own, keys_own, values_own, marks_own, attention_own, cot_own
    )
    grads_own = jnp.concatenate([grad_q, grad_k, grad_v], axis=2).reshape(
        heads_local, ctx_count, capacity, 3 * HD
    )
    grads_back = lax.all_to_all(grads_own, "ctx", split_axis=1, concat_axis=1, tiled=True)
    grad_heads = unpack(grads_back)
    attention_rows = jnp.transpose(attention_tok, (1, 0, 2)).reshape(tok_count, heads_local * HD)
    out_terms = jnp.dot(attention_rows, w_out, preferred_element_type=jnp.float32)
    attended = lax.psum_scatter(
        out_terms.astype(jnp.bfloat16), "tensor", scatter_dimension=1, tiled=True
    )
    grad_qkv = jnp.transpose(grad_heads.reshape(heads_local, tok_count, 3, HD), (1, 2, 0, 3))
    grad_qkv = grad_qkv.reshape(tok_count, 3 * heads_local * HD)
    grad_w_out_local = contract_first(attention_rows, tok_grads)
    grad_w_qkv_local = contract_first(tok_rows, grad_qkv).reshape(width, 3, heads_local * HD)
    summed_qkv, summed_out = (
        lax.psum(grad_w_qkv_local.astype(jnp.bfloat16), ("ctx", "dp")).astype(jnp.float32),
        lax.psum(grad_w_out_local.astype(jnp.bfloat16), ("ctx", "dp")).astype(jnp.float32),
    )
    in_terms = contract_last(grad_qkv, w_qkv.reshape(width, 3 * heads_local * HD))
    grad_tokens = lax.psum_scatter(
        in_terms.astype(jnp.bfloat16), "tensor", scatter_dimension=1, tiled=True
    )
    return (attended[None], grad_tokens[None], summed_qkv, summed_out)


def solution(mesh):
    placed = (
        P(("groups", "dp"), "ctx", "tensor"),
        P(None, None, "tensor"),
        P("tensor", None),
        P(("groups", "dp"), "tensor", "ctx"),
        P(("groups", "dp"), "ctx", "tensor"),
    )
    return jax.shard_map(
        shards,
        mesh=mesh,
        in_specs=placed,
        out_specs=(
            P(("groups", "dp"), "ctx", "tensor"),
            P(("groups", "dp"), "ctx", "tensor"),
            P("groups", None, "tensor"),
            P(("groups", "tensor"), None),
        ),
        check_vma=False,
    )
```

profile of v0, /device:TPU:0, one launch (start us, length us, event | category | flops | bytes accessed | tf_op | source)
XLA Modules:
  0.0 419.2 jit_solution(18375576288930993019)
XLA Ops:
  10.2 4.8 %reduce-window.6 = s32[4,4,2,128]{3,2,1,0:T(2,128)S(1)} reduce-window(s32[4,4,2,128]{3,2,1,0:T(2,128)S(1)} %compare_convert_fusion, s32[]{:T(128)} %constant.96.clone.1), window={size=1x1x1x128 pad=0_0x0_0x0_0x127_0}, to_apply=%region_0.1 | reduce-window | flops 520192 | bytes 32772 | tf_op jit(solution)/shard_map/reduce-window
  17.8 7.6 %scatter_custom_fusion = bf16[3072]{0:T(1024)(128)(2,1)S(1)} fusion(s32[1024]{0:T(1024)S(1)} %bitcast.228, bf16[1024]{0:T(1024)(128)(2,1)S(1)} %bitcast.231, bf16[]{:T(256)} %constant.103.clone.1), kind=kCustom, calls=%fused_computation.120 | custom fusion | bytes 6146
  26.1 6.3 %all-to-all-start = ((bf16[4,4,192]{2,0,1:T(4,128)(2,1)}), bf16[4,4,192]{2,0,1:T(4,128)(2,1)S(1)}, u32[]{:S(2)}, u32[]{:S(2)}) async-start(bf16[4,4,192]{2,0,1:T(4,128)(2,1)} %copy.67), calls=%async_computation | async-start | bytes 16384 | tf_op jit(solution)/shard_map/all_to_all | solution.py:132
  32.4 8.6 %all_gather.7 = bf16[1,256,1024]{2,1,0:T(8,128)(2,1)S(1)} all-gather(bf16[1,256,512]{2,1,0:T(8,128)(2,1)} %param.13), channel_id=1, replica_groups=mesh['groups'=2,'ctx'=4,'tensor'=2,'dp'=2] {'tensor'}, dimensions={2}, use_global_device_ids=true | all-gather | bytes 786432 | tf_op jit(solution)/shard_map/all_gather | solution.py:88
  42.4 3.4 scatter_custom_fusion.2
  46.8 4.8 %all-to-all-start.3 = ((bf16[4,4,192,128]{3,2,0,1:T(8,128)(2,1)}), bf16[4,4,192,128]{3,2,0,1:T(8,128)(2,1)}, u32[]{:S(2)}, u32[]{:S(2)}) async-start(bf16[4,4,192,128]{3,2,0,1:T(8,128)(2,1)} %copy.80), calls=%async_computation.4 | async-start | bytes 1572864 | tf_op jit(solution)/shard_map/all_to_all | solution.py:148
  51.6 4.7 %copy.69 = bf16[1024,3,512]{0,2,1:T(8,128)(2,1)} copy(bf16[1024,3,512]{2,0,1:T(8,128)(2,1)} %param.10) | data formatting | bytes 6291456 | tf_op args[1]
  56.3 7.0 %all_gather.6 = bf16[1,256,1024]{2,1,0:T(8,128)(2,1)S(1)} all-gather(bf16[1,256,512]{2,1,0:T(8,128)(2,1)S(1)} %copy-done.10), channel_id=1, replica_groups=mesh['groups'=2,'ctx'=4,'tensor'=2,'dp'=2] {'tensor'}, dimensions={2}, use_global_device_ids=true | all-gather | bytes 786432 | tf_op jit(solution)/shard_map/all_gather | solution.py:87
  69.3 6.5 %scatter_custom_fusion.1 = bf16[3072,384]{1,0:T(8,128)(2,1)S(1)} fusion(s32[1024]{0:T(1024)S(1)} %bitcast.230, bf16[1024,384]{1,0:T(8,128)(2,1)} %copy.71, bf16[]{:T(256)} %constant.102.clone.1), kind=kCustom, calls=%fused_computation.77 | custom fusion | bytes 2359808
  77.5 5.1 %all-to-all-start.1 = ((bf16[4,4,192,384]{3,2,0,1:T(8,128)(2,1)}), bf16[4,4,192,384]{3,2,0,1:T(8,128)(2,1)}, u32[]{:S(2)}, u32[]{:S(2)}) async-start(bf16[4,4,192,384]{3,2,0,1:T(8,128)(2,1)} %copy.72), calls=%async_computation.1 | async-start | bytes 4718592 | tf_op jit(solution)/shard_map/all_to_all | solution.py:131
  85.0 48.7 %all-to-all-done.1 = bf16[4,4,192,384]{3,2,0,1:T(8,128)(2,1)} async-done(((bf16[4,4,192,384]{3,2,0,1:T(8,128)(2,1)}), bf16[4,4,192,384]{3,2,0,1:T(8,128)(2,1)}, u32[]{:S(2)}, u32[]{:S(2)}) %all-to-all-start.1) | async-done | bytes 2359328 | tf_op jit(solution)/shard_map/all_to_all | solution.py:131
  137.4 23.0 %while.33 = (s32[]{:T(128)}, bf16[3,4,256,128]{3,2,0,1:T(8,128)(2,1)S(1)}, s32[3]{0:T(128)S(1)}, bf16[4,768]{1,0:T(4,128)(2,1)S(1)}, bf16[4,4,192]{2,1,0:T(4,128...) while((s32[]{:T(128)}, ...), condition=%wide.wide.region_8.9_spmd, body=%wide.wide.region_5.8_spmd.sunk | while | flops 612764160 | bytes 3175139 | solution.py:43
  141.3 3.8 fusion.173
  149.0 3.8 fusion.173
  156.6 3.8 fusion.173
  161.4 4.2 all-to-all-start.2
  166.7 56.3 %while.34 = (s32[]{:T(128)}, f32[4,768,128]{2,1,0:T(8,128)S(1)}, f32[4,768,128]{2,1,0:T(8,128)}, bf16[3,4,256,128]{3,2,0,1:T(8,128)(2,1)}, s32[3]{0:T(128)S(1)},...) while((s32[]{:T(128)}, f32[4,768,128]{2,1,0:T(8,128)S(1)}, ...), condition=%wide.wide.region_15.16_spmd.clone, body=%wide.wide.region_11.15_spmd.clone.sunk | while | flops 1222772224 | bytes 25732404 | solution.py:75
  169.2 4.1 fusion.187
  179.9 5.2 %select_add_fusion.7 = f32[4,768,128]{2,1,0:T(8,128)} fusion(f32[4,768,128]{2,1,0:T(8,128)} %get-tuple-element.590, f32[4,256]{1,0:T(4,128)S(1)} %get-tuple-element.527, pred[]{:T(512)S(6)} %compare.29, bf16[4,768,128]{2,1,0:T(8,128)(2,1)} %get-tuple-element.615, s32[]{:T(128)S(1)} %bitcast.226, ...), kind=kOutput, calls=%fused_computation.37.clone.clone.1 | convolution fusion | flops 408160000 | bytes 4469761 | tf_op jit(solution)/shard_map/vmap()/while/body/eval_jaxpr/dot_general | solution.py:17
  187.6 4.1 fusion.187
  191.7 3.0 multiply_convert_fusion.3
  198.3 5.7 %select_add_fusion.7 = f32[4,768,128]{2,1,0:T(8,128)} fusion(f32[4,768,128]{2,1,0:T(8,128)} %get-tuple-element.590, f32[4,256]{1,0:T(4,128)S(1)} %get-tuple-element.527, pred[]{:T(512)S(6)} %compare.29, bf16[4,768,128]{2,1,0:T(8,128)(2,1)} %get-tuple-element.615, s32[]{:T(128)S(1)} %bitcast.226, ...), kind=kOutput, calls=%fused_computation.37.clone.clone.1 | convolution fusion | flops 408160000 | bytes 4469761 | tf_op jit(solution)/shard_map/vmap()/while/body/eval_jaxpr/dot_general | solution.py:17
  206.6 4.1 fusion.187
  217.2 5.7 %select_add_fusion.7 = f32[4,768,128]{2,1,0:T(8,128)} fusion(f32[4,768,128]{2,1,0:T(8,128)} %get-tuple-element.590, f32[4,256]{1,0:T(4,128)S(1)} %get-tuple-element.527, pred[]{:T(512)S(6)} %compare.29, bf16[4,768,128]{2,1,0:T(8,128)(2,1)} %get-tuple-element.615, s32[]{:T(128)S(1)} %bitcast.226, ...), kind=kOutput, calls=%fused_computation.37.clone.clone.1 | convolution fusion | flops 408160000 | bytes 4469761 | tf_op jit(solution)/shard_map/vmap()/while/body/eval_jaxpr/dot_general | solution.py:17
  227.6 5.2 %all-to-all-start.4 = ((bf16[4,4,192,384]{3,2,0,1:T(8,128)(2,1)}), bf16[4,4,192,384]{3,2,0,1:T(8,128)(2,1)}, u32[]{:S(2)}, u32[]{:S(2)}) async-start(bf16[4,4,192,384]{3,2,0,1:T(8,128)(2,1)} %copy.84), calls=%async_computation.5 | async-start | bytes 4718592 | tf_op jit(solution)/shard_map/all_to_all | solution.py:156
  234.1 5.8 %gather_fusion = bf16[1024,128]{1,0:T(8,128)(2,1)S(1)} fusion(bf16[4,768,128]{2,1,0:T(8,128)(2,1)S(1)} %bitcast.205, s32[1024]{0:T(1024)S(1)} %bitcast.199), kind=kCustom, calls=%fused_computation | custom fusion | bytes 532480 | tf_op jit(solution)/shard_map/vmap(jit(_take))/gather | solution.py:123
  242.3 43.4 %all-to-all-done.4 = bf16[4,4,192,384]{3,2,0,1:T(8,128)(2,1)} async-done(((bf16[4,4,192,384]{3,2,0,1:T(8,128)(2,1)}), bf16[4,4,192,384]{3,2,0,1:T(8,128)(2,1)}, u32[]{:S(2)}, u32[]{:S(2)}) %all-to-all-start.4) | async-done | bytes 2359328 | tf_op jit(solution)/shard_map/all_to_all | solution.py:156
  287.6 11.6 %gather_fusion.1 = bf16[1024,384]{1,0:T(8,128)(2,1)} fusion(bf16[4,768,384]{2,1,0:T(8,128)(2,1)S(1)} %bitcast.201, s32[1024]{0:T(1024)S(1)} %bitcast.200), kind=kCustom, calls=%fused_computation.1 | custom fusion | bytes 1581056 | tf_op jit(solution)/shard_map/vmap(jit(_take))/gather | solution.py:123
  304.4 4.7 %copy.88 = bf16[1024,3,512]{2,0,1:T(8,128)(2,1)} copy(bf16[1024,3,512]{0,2,1:T(8,128)(2,1)} %bitcast.202) | data formatting | bytes 6291456 | tf_op jit(solution)/shard_map/convert_element_type | solution.py:168
  311.3 3.7 convolution_convert_fusion.5
  315.1 90.2 %all-reduce.3.cloned.1.call-done = (bf16[1024,3,512]{2,0,1:T(8,128)(2,1)}, bf16[512,1024]{1,0:T(8,128)(2,1)}) async-done(((bf16[1024,3,512]{2,0,1:T(8,128)(2,1)}, bf16[512,1024]{1,0:T(8,128)(2,1)}), (bf16[1024,3,512]{2,0,1:T(8,128)(2,1)}, bf16[512,1024]{1,0:T(8,128)(2,1)})) %all-reduce.3.cloned.1.call-update) | async-done | bytes 4194320 | tf_op jit(solution)/shard_map/psum | solution.py:168
  408.2 3.6 convert_element_type.79
  (136 shorter events, 75.9 us)
Async XLA Ops:
  8.0 33.8 %copy-start = (bf16[512,1024]{1,0:T(8,128)(2,1)S(1)}, bf16[512,1024]{1,0:T(8,128)(2,1)}, u32[]{:S(2)}) copy-start(bf16[512,1024]{1,0:T(8,128)(2,1)} %param.11) | copy-start | bytes 3145732
  26.1 20.7 %all-to-all-start = ((bf16[4,4,192]{2,0,1:T(4,128)(2,1)}), bf16[4,4,192]{2,0,1:T(4,128)(2,1)S(1)}, u32[]{:S(2)}, u32[]{:S(2)}) async-start(bf16[4,4,192]{2,0,1:T(4,128)(2,1)} %copy.67), calls=%async_computation | async-start | bytes 16384 | tf_op jit(solution)/shard_map/all_to_all | solution.py:132
  41.0 0.8 copy-start.1
  46.8 30.7 %all-to-all-start.3 = ((bf16[4,4,192,128]{3,2,0,1:T(8,128)(2,1)}), bf16[4,4,192,128]{3,2,0,1:T(8,128)(2,1)}, u32[]{:S(2)}, u32[]{:S(2)}) async-start(bf16[4,4,192,128]{3,2,0,1:T(8,128)(2,1)} %copy.80), calls=%async_computation.4 | async-start | bytes 1572864 | tf_op jit(solution)/shard_map/all_to_all | solution.py:148
  51.6 4.7 %copy-start.10 = (bf16[1,256,512]{2,1,0:T(8,128)(2,1)S(1)}, bf16[1,256,512]{2,1,0:T(8,128)(2,1)}, u32[]{:S(2)}) copy-start(bf16[1,256,512]{2,1,0:T(8,128)(2,1)} %param.9) | copy-start | bytes 786436
  63.3 0.8 copy-start.6
  77.5 56.2 %all-to-all-start.1 = ((bf16[4,4,192,384]{3,2,0,1:T(8,128)(2,1)}), bf16[4,4,192,384]{3,2,0,1:T(8,128)(2,1)}, u32[]{:S(2)}, u32[]{:S(2)}) async-start(bf16[4,4,192,384]{3,2,0,1:T(8,128)(2,1)} %copy.72), calls=%async_computation.1 | async-start | bytes 4718592 | tf_op jit(solution)/shard_map/all_to_all | solution.py:131
  82.6 53.0 %copy-start.11 = (bf16[4,4,192]{2,1,0:T(4,128)(2,1)}, bf16[4,4,192]{2,1,0:T(4,128)(2,1)S(1)}, u32[]{:S(2)}) copy-start(bf16[4,4,192]{2,1,0:T(4,128)(2,1)S(1)} %copy.68) | copy-start | bytes 18436
  161.4 66.2 %all-to-all-start.2 = ((bf16[4,4,192,128]{3,2,0,1:T(8,128)(2,1)}), bf16[4,4,192,128]{3,2,0,1:T(8,128)(2,1)}, u32[]{:S(2)}, u32[]{:S(2)}) async-start(bf16[4,4,192,128]{3,2,0,1:T(8,128)(2,1)} %copy.76), calls=%async_computation.2 | async-start | bytes 1572864 | tf_op jit(solution)/shard_map/all_to_all | solution.py:140
  173.3 3.0 copy-start.9
  191.7 3.0 copy-start.9
  210.7 3.0 copy-start.9
  223.0 1.4 copy-start.8
  227.6 5.2 %copy-start.12 = (s32[1,4,256]{2,1,0:T(4,128)S(1)}, s32[1,4,256]{2,1,0:T(4,128)}, u32[]{:S(2)}) copy-start(s32[1,4,256]{2,1,0:T(4,128)} %param.12) | copy-start | bytes 12292
  227.6 58.0 %all-to-all-start.4 = ((bf16[4,4,192,384]{3,2,0,1:T(8,128)(2,1)}), bf16[4,4,192,384]{3,2,0,1:T(8,128)(2,1)}, u32[]{:S(2)}, u32[]{:S(2)}) async-start(bf16[4,4,192,384]{3,2,0,1:T(8,128)(2,1)} %copy.84), calls=%async_computation.5 | async-start | bytes 4718592 | tf_op jit(solution)/shard_map/all_to_all | solution.py:156
  232.8 8.0 %copy-start.2 = (bf16[1,256,1024]{2,1,0:T(8,128)(2,1)S(1)}, bf16[1,256,1024]{2,1,0:T(8,128)(2,1)}, u32[]{:S(2)}) copy-start(bf16[1,256,1024]{2,1,0:T(8,128)(2,1)} %copy-done.1) | copy-start | bytes 1572868
  232.8 172.4 %all-reduce.3.cloned.1.call-start = ((), (), s32[]{:S(2)}) async-start(), calls=%async_computation.9 | async-start | bytes 8388608 | tf_op jit(solution)/shard_map/psum | solution.py:168
  240.2 0.7 copy-start.4
  299.2 2.5 copy-start.7
  309.1 0.9 copy-start.5
  309.1 102.7 %reduce-scatter.3.cloned.1.call-start = ((), (), s32[]{:S(2)}) async-start(), calls=%async_computation.7 | async-start | bytes 786432 | tf_op jit(solution)/shard_map/reduce_scatter | solution.py:160
  311.3 100.5 %reduce-scatter.5.cloned.1.call-start = ((), (), s32[]{:S(2)}) async-start(), calls=%async_computation.8 | async-start | bytes 786432 | tf_op jit(solution)/shard_map/reduce_scatter | solution.py:172
  405.2 2.9 copy-start.3
Sparse Core Ops, SparseCore 0:
  309.2 95.9 all-reduce.2
Sparse Core Ops, SparseCore 1:
  312.4 13.6 reduce-scatter.2
  328.8 14.5 reduce-scatter.4
where the time goes:
time: 421 us; the launch traced here: 419 us
  waiting for transfers between devices  182 us (43%)
  matrix products  80 us (19%)
  local copies, waits for them, and re-layouts  74.3 us (18%)
  starting transfers between devices  25.7 us (6%)
  other arithmetic  21.4 us (5%)
  between operations  15.8 us (4%)
  blocking collectives  15.7 us (4%)
    psum x1, waiting for transfers between devices, shards(): lax.psum(grad_w_qkv_local.astype(jnp.bfloat16), ('ctx', 'dp'))  90.2 us
    all_to_all x1, waiting for transfers between devices, shards(): lax.all_to_all(pack(qkv_heads), 'ctx', split_axis=1, concat_axis=1, tiled...  48.7 us
    all_to_all x1, waiting for transfers between devices, shards(): lax.all_to_all(grads_own, 'ctx', split_axis=1, concat_axis=1, tiled=True)  43.4 us
    dot_general x8, matrix products, contract_first(): lax.dot_general(left, right, (((0,), (0,)), ((), ())), preferred_element_...  27.5 us
    unnamed x32, local copies, waits for them, and re-layouts  26.9 us
    sub x6, matrix products, masked_probs(): expo = jnp.exp(scores - top_value)  19.8 us
    gather x5, local copies, waits for them, and re-layouts, unpack(): jnp.take(table, where_to, axis=0)  19.6 us
    dot_general x5, matrix products, contract_last(): lax.dot_general(left, right, (((1,), (1,)), ((), ())), preferred_element_...  13.2 us
  transfers between devices with their start and end apart: 8, of which 3 were waited for; matrix products, arithmetic and copies ran while one was open for 25% of the time, Pallas kernels for 0%

commit v1 on v0

--- a/solution.py
+++ b/solution.py
@@ -1,3 +1,4 @@
+import functools
 import math
 import jax
 import jax.numpy as jnp
@@ -5,6 +6,38 @@
 from jax.sharding import PartitionSpec as P
 
 HD = 128
+
+
+def raise_spans(packet, array_dim, page):
+    value_now = packet.shape
+    reply = packet.reshape(
+        *value_now[:array_dim], page, value_now[array_dim] // page, *value_now[array_dim + 1 :]
+    )
+    return jnp.moveaxis(reply, array_dim, 0)
+
+
+def follow_trails_now(obj, out_dim):
+    vec_out = list(obj.shape[1:])
+    vec_out[out_dim] *= obj.shape[0]
+    return jnp.moveaxis(obj, 0, out_dim).reshape(vec_out)
+
+
+def do_rows_all(u, row_axis, patch, mine_x):
+    arr_now, all_rows = (lax.axis_size(row_axis), lax.axis_index(row_axis))
+    part_now = raise_spans(u, patch, arr_now)
+    j = 1
+    by_place = [part_now[all_rows]]
+    while j < arr_now:
+        fresh = part_now[all_rows ^ j]
+        by_place.append(
+            lax.ppermute(fresh, axis_name=row_axis, perm=[(rr, rr ^ j) for rr in range(arr_now)])
+        )
+        j += 1
+    part_now = jnp.stack(by_place)[all_rows ^ jnp.arange(arr_now)]
+    return follow_trails_now(part_now, mine_x)
+
+
+sector_meet = functools.partial(do_rows_all, row_axis="ctx", patch=1, mine_x=1)
 
 
 def contract_last(left, right):
@@ -128,7 +161,7 @@
         lambda where_to, marks: jnp.full((slot_total,), -1.0, jnp.bfloat16).at[where_to].set(marks)
     )(destination, labels_local.astype(jnp.bfloat16)).reshape(heads_local, ctx_count, capacity)
     arrived, arrived_marks = (
-        lax.all_to_all(pack(qkv_heads), "ctx", split_axis=1, concat_axis=1, tiled=True),
+        sector_meet(pack(qkv_heads)),
         lax.all_to_all(label_slots, "ctx", split_axis=1, concat_axis=1, tiled=True),
     )
     arrived = arrived.reshape(heads_local, slot_total, 3 * HD)

time: 421 us -> 400 us (0.950)
  waiting for transfers between devices: 182 us -> 156 us
    all_to_all x1 -> x0, waiting for transfers between devices: 48.7 us -> none  [shards(): lax.all_to_all(pack(qkv_heads), 'ctx', split_axis=1, concat_axis=1, tiled...]
    all_to_all x1, waiting for transfers between devices: 0.01 us -> 21.7 us  [shards(): lax.all_to_all(label_slots, 'ctx', split_axis=1, concat_axis=1, tiled=True)]
    all_to_all x1 -> x0, starting transfers between devices: 5.09 us -> none  [shards(): lax.all_to_all(pack(qkv_heads), 'ctx', split_axis=1, concat_axis=1, tiled...]
    ppermute x0 -> x3, starting transfers between devices: none -> 4.39 us  [do_rows_all(): lax.ppermute(fresh, axis_name=row_axis, perm=[(rr, rr ^ j) for rr in rang...]
    unnamed x32 -> x30, local copies, waits for them, and re-layouts: 26.9 us -> 25.7 us
  transfers between devices with their start and end apart: 8 -> 10, of which waited for: 3 -> 3; matrix products, arithmetic and copies ran while one was open for 25% -> 32% of each run, Pallas kernels for 0% -> 0%
where the time goes in v1:
time: 400 us; the launch traced here: 398 us
  waiting for transfers between devices  156 us (39%)
  matrix products  79.9 us (20%)
  local copies, waits for them, and re-layouts  77.3 us (19%)
  other arithmetic  24.1 us (6%)
  starting transfers between devices  23.9 us (6%)
  blocking collectives  17.6 us (4%)
  between operations  15.8 us (4%)
  loops' own time  4.09 us (1%)
    psum x1, waiting for transfers between devices, shards(): lax.psum(grad_w_qkv_local.astype(jnp.bfloat16), ('ctx', 'dp'))  90.2 us
    all_to_all x1, waiting for transfers between devices, shards(): lax.all_to_all(grads_own, 'ctx', split_axis=1, concat_axis=1, tiled=True)  43.6 us
    dot_general x8, matrix products, contract_first(): lax.dot_general(left, right, (((0,), (0,)), ((), ())), preferred_element_...  27.4 us
    unnamed x30, local copies, waits for them, and re-layouts  25.7 us
    all_to_all x1, waiting for transfers between devices, shards(): lax.all_to_all(label_slots, 'ctx', split_axis=1, concat_axis=1, tiled=True)  21.7 us
    sub x6, matrix products, masked_probs(): expo = jnp.exp(scores - top_value)  19.8 us
    gather x5, local copies, waits for them, and re-layouts, unpack(): jnp.take(table, where_to, axis=0)  19.5 us
    dot_general x5, matrix products, contract_last(): lax.dot_general(left, right, (((1,), (1,)), ((), ())), preferred_element_...  13.2 us
  transfers between devices with their start and end apart: 10, of which 3 were waited for; matrix products, arithmetic and copies ran while one was open for 32% of the time, Pallas kernels for 0%

profile of v1, /device:TPU:0, one launch (start us, length us, event | category | flops | bytes accessed | tf_op | source)
XLA Modules:
  0.0 398.3 jit_solution(16426957476552359317)
XLA Ops:
  9.5 4.8 %reduce-window.6 = s32[4,4,2,128]{3,2,1,0:T(2,128)S(1)} reduce-window(s32[4,4,2,128]{3,2,1,0:T(2,128)S(1)} %compare_convert_fusion, s32[]{:T(128)} %constant.82.clone.1), window={size=1x1x1x128 pad=0_0x0_0x0_0x127_0}, to_apply=%region_0.1 | reduce-window | flops 520192 | bytes 32772 | tf_op jit(solution)/shard_map/reduce-window
  17.1 10.2 %all_gather.6 = bf16[1,256,1024]{2,1,0:T(8,128)(2,1)S(1)} all-gather(bf16[1,256,512]{2,1,0:T(8,128)(2,1)} %param.9), channel_id=1, replica_groups=mesh['groups'=2,'ctx'=4,'tensor'=2,'dp'=2] {'tensor'}, dimensions={2}, use_global_device_ids=true | all-gather | bytes 786432 | tf_op jit(solution)/shard_map/all_gather | solution.py:120
  27.3 4.8 %copy.70 = bf16[1024,3,512]{0,2,1:T(8,128)(2,1)} copy(bf16[1024,3,512]{2,0,1:T(8,128)(2,1)} %param.10) | data formatting | bytes 6291456 | tf_op args[1]
  37.3 6.3 %scatter_custom_fusion.1 = bf16[3072,384]{1,0:T(8,128)(2,1)S(1)} fusion(s32[1024]{0:T(1024)S(1)} %bitcast.247, bf16[1024,384]{1,0:T(8,128)(2,1)} %copy.72, bf16[]{:T(256)} %constant.110.clone.1), kind=kCustom, calls=%fused_computation.79 | custom fusion | bytes 2359808
  45.1 3.8 collective-permute-start.2
  49.5 7.6 %scatter_custom_fusion = bf16[3072]{0:T(1024)(128)(2,1)S(1)} fusion(s32[1024]{0:T(1024)S(1)} %bitcast.248, bf16[1024]{0:T(1024)(128)(2,1)S(1)} %bitcast.250, bf16[]{:T(256)} %constant.115.clone.1), kind=kCustom, calls=%fused_computation.127 | custom fusion | bytes 6146
  57.8 5.1 %all-to-all-start = ((bf16[4,4,192]{2,0,1:T(4,128)(2,1)}), bf16[4,4,192]{2,0,1:T(4,128)(2,1)S(1)}, u32[]{:S(2)}, u32[]{:S(2)}) async-start(bf16[4,4,192]{2,0,1:T(4,128)(2,1)} %copy.68), calls=%async_computation | async-start | bytes 16384 | tf_op jit(solution)/shard_map/all_to_all | solution.py:165
  62.9 7.4 %all_gather.7 = bf16[1,256,1024]{2,1,0:T(8,128)(2,1)S(1)} all-gather(bf16[1,256,512]{2,1,0:T(8,128)(2,1)} %param.13), channel_id=1, replica_groups=mesh['groups'=2,'ctx'=4,'tensor'=2,'dp'=2] {'tensor'}, dimensions={2}, use_global_device_ids=true | all-gather | bytes 786432 | tf_op jit(solution)/shard_map/all_gather | solution.py:121
  72.4 3.8 scatter_custom_fusion.2
  77.2 21.7 %all-to-all-done = bf16[4,4,192]{2,0,1:T(4,128)(2,1)S(1)} async-done(((bf16[4,4,192]{2,0,1:T(4,128)(2,1)}), bf16[4,4,192]{2,0,1:T(4,128)(2,1)S(1)}, u32[]{:S(2)}, u32[]{:S(2)}) %all-to-all-start) | async-done | bytes 6176 | tf_op jit(solution)/shard_map/all_to_all | solution.py:165
  98.9 4.2 %all-to-all-start.2 = ((bf16[4,4,192,128]{3,2,0,1:T(8,128)(2,1)}), bf16[4,4,192,128]{3,2,0,1:T(8,128)(2,1)}, u32[]{:S(2)}, u32[]{:S(2)}) async-start(bf16[4,4,192,128]{3,2,0,1:T(8,128)(2,1)} %copy.80), calls=%async_computation.3 | async-start | bytes 1572864 | tf_op jit(solution)/shard_map/all_to_all | solution.py:181
  106.7 3.9 gather_fusion
  114.3 23.0 %while.33 = (s32[]{:T(128)}, bf16[3,4,256,128]{3,2,0,1:T(8,128)(2,1)S(1)}, s32[3]{0:T(128)S(1)}, bf16[4,768]{1,0:T(4,128)(2,1)S(1)}, bf16[4,4,192]{2,1,0:T(4,128...) while((s32[]{:T(128)}, ...), condition=%wide.wide.region_8.9_spmd, body=%wide.wide.region_5.8_spmd.sunk | while | flops 612764160 | bytes 3175139 | solution.py:76
  118.2 3.8 fusion.174
  125.9 3.8 fusion.174
  133.5 3.8 fusion.174
  138.3 5.0 %all-to-all-start.1 = ((bf16[4,4,192,128]{3,2,0,1:T(8,128)(2,1)}), bf16[4,4,192,128]{3,2,0,1:T(8,128)(2,1)}, u32[]{:S(2)}, u32[]{:S(2)}) async-start(bf16[4,4,192,128]{3,2,0,1:T(8,128)(2,1)} %copy.76), calls=%async_computation.1 | async-start | bytes 1572864 | tf_op jit(solution)/shard_map/all_to_all | solution.py:173
  146.5 56.2 %while.34 = (s32[]{:T(128)}, f32[4,768,128]{2,1,0:T(8,128)S(1)}, f32[4,768,128]{2,1,0:T(8,128)}, bf16[3,4,256,128]{3,2,0,1:T(8,128)(2,1)}, s32[3]{0:T(128)S(1)},...) while((s32[]{:T(128)}, f32[4,768,128]{2,1,0:T(8,128)S(1)}, ...), condition=%wide.wide.region_15.16_spmd.clone, body=%wide.wide.region_11.15_spmd.clone.sunk | while | flops 1222772224 | bytes 25732404 | solution.py:108
  149.0 4.1 %fusion.188 = (f32[4,256]{1,0:T(4,128)S(1)}, f32[4,256,768]{2,1,0:T(8,128)}) fusion(bf16[4,256]{1,0:T(4,128)(2,1)S(1)} %constant_dynamic-slice_fusion.7, bf16[4,768]{1,0:T(4,128)(2,1)S(1)} %get-tuple-element.622, bf16[4,768,128]{2,1,0:T(8,128)(2,1)} %get-tuple-element.618, bf16[4,768,128]{2,1,0:T(8,128)(2,1)} %get-tuple-element.617, ...), kind=kOutput, calls=%fused_computation.133.clone.clone.1 | convolution fusion | flops 205259520 | bytes 4206596 | tf_op jit(solution)/shard_map/vmap()/while/body/eval_jaxpr/sub | solution.py:60
  159.7 5.2 %select_add_fusion.7 = f32[4,768,128]{2,1,0:T(8,128)} fusion(f32[4,768,128]{2,1,0:T(8,128)} %get-tuple-element.594, f32[4,256]{1,0:T(4,128)S(1)} %get-tuple-element.531, pred[]{:T(512)S(6)} %compare.29, bf16[4,768,128]{2,1,0:T(8,128)(2,1)} %get-tuple-element.619, s32[]{:T(128)S(1)} %bitcast.245, ...), kind=kOutput, calls=%fused_computation.38.clone.clone.1 | convolution fusion | flops 408160000 | bytes 4469761 | tf_op jit(solution)/shard_map/vmap()/while/body/eval_jaxpr/dot_general | solution.py:50
  167.4 4.1 %fusion.188 = (f32[4,256]{1,0:T(4,128)S(1)}, f32[4,256,768]{2,1,0:T(8,128)}) fusion(bf16[4,256]{1,0:T(4,128)(2,1)S(1)} %constant_dynamic-slice_fusion.7, bf16[4,768]{1,0:T(4,128)(2,1)S(1)} %get-tuple-element.622, bf16[4,768,128]{2,1,0:T(8,128)(2,1)} %get-tuple-element.618, bf16[4,768,128]{2,1,0:T(8,128)(2,1)} %get-tuple-element.617, ...), kind=kOutput, calls=%fused_computation.133.clone.clone.1 | convolution fusion | flops 205259520 | bytes 4206596 | tf_op jit(solution)/shard_map/vmap()/while/body/eval_jaxpr/sub | solution.py:60
  178.0 5.7 %select_add_fusion.7 = f32[4,768,128]{2,1,0:T(8,128)} fusion(f32[4,768,128]{2,1,0:T(8,128)} %get-tuple-element.594, f32[4,256]{1,0:T(4,128)S(1)} %get-tuple-element.531, pred[]{:T(512)S(6)} %compare.29, bf16[4,768,128]{2,1,0:T(8,128)(2,1)} %get-tuple-element.619, s32[]{:T(128)S(1)} %bitcast.245, ...), kind=kOutput, calls=%fused_computation.38.clone.clone.1 | convolution fusion | flops 408160000 | bytes 4469761 | tf_op jit(solution)/shard_map/vmap()/while/body/eval_jaxpr/dot_general | solution.py:50
  186.3 4.1 %fusion.188 = (f32[4,256]{1,0:T(4,128)S(1)}, f32[4,256,768]{2,1,0:T(8,128)}) fusion(bf16[4,256]{1,0:T(4,128)(2,1)S(1)} %constant_dynamic-slice_fusion.7, bf16[4,768]{1,0:T(4,128)(2,1)S(1)} %get-tuple-element.622, bf16[4,768,128]{2,1,0:T(8,128)(2,1)} %get-tuple-element.618, bf16[4,768,128]{2,1,0:T(8,128)(2,1)} %get-tuple-element.617, ...), kind=kOutput, calls=%fused_computation.133.clone.clone.1 | convolution fusion | flops 205259520 | bytes 4206596 | tf_op jit(solution)/shard_map/vmap()/while/body/eval_jaxpr/sub | solution.py:60
  196.9 5.7 %select_add_fusion.7 = f32[4,768,128]{2,1,0:T(8,128)} fusion(f32[4,768,128]{2,1,0:T(8,128)} %get-tuple-element.594, f32[4,256]{1,0:T(4,128)S(1)} %get-tuple-element.531, pred[]{:T(512)S(6)} %compare.29, bf16[4,768,128]{2,1,0:T(8,128)(2,1)} %get-tuple-element.619, s32[]{:T(128)S(1)} %bitcast.245, ...), kind=kOutput, calls=%fused_computation.38.clone.clone.1 | convolution fusion | flops 408160000 | bytes 4469761 | tf_op jit(solution)/shard_map/vmap()/while/body/eval_jaxpr/dot_general | solution.py:50
  207.4 5.1 %all-to-all-start.3 = ((bf16[4,4,192,384]{3,2,0,1:T(8,128)(2,1)}), bf16[4,4,192,384]{3,2,0,1:T(8,128)(2,1)}, u32[]{:S(2)}, u32[]{:S(2)}) async-start(bf16[4,4,192,384]{3,2,0,1:T(8,128)(2,1)} %copy.84), calls=%async_computation.4 | async-start | bytes 4718592 | tf_op jit(solution)/shard_map/all_to_all | solution.py:189
  213.7 5.8 %gather_fusion.1 = bf16[1024,128]{1,0:T(8,128)(2,1)S(1)} fusion(bf16[4,768,128]{2,1,0:T(8,128)(2,1)S(1)} %bitcast.223, s32[1024]{0:T(1024)S(1)} %bitcast.217), kind=kCustom, calls=%fused_computation.1 | custom fusion | bytes 532480 | tf_op jit(solution)/shard_map/vmap(jit(_take))/gather | solution.py:156
  221.2 43.6 %all-to-all-done.3 = bf16[4,4,192,384]{3,2,0,1:T(8,128)(2,1)} async-done(((bf16[4,4,192,384]{3,2,0,1:T(8,128)(2,1)}), bf16[4,4,192,384]{3,2,0,1:T(8,128)(2,1)}, u32[]{:S(2)}, u32[]{:S(2)}) %all-to-all-start.3) | async-done | bytes 2359328 | tf_op jit(solution)/shard_map/all_to_all | solution.py:189
  266.7 11.6 %gather_fusion.2 = bf16[1024,384]{1,0:T(8,128)(2,1)} fusion(bf16[4,768,384]{2,1,0:T(8,128)(2,1)S(1)} %bitcast.219, s32[1024]{0:T(1024)S(1)} %bitcast.218), kind=kCustom, calls=%fused_computation.2 | custom fusion | bytes 1581056 | tf_op jit(solution)/shard_map/vmap(jit(_take))/gather | solution.py:156
  283.5 4.7 %copy.88 = bf16[1024,3,512]{2,0,1:T(8,128)(2,1)} copy(bf16[1024,3,512]{0,2,1:T(8,128)(2,1)} %bitcast.220) | data formatting | bytes 6291456 | tf_op jit(solution)/shard_map/convert_element_type | solution.py:201
  290.4 3.7 convolution_convert_fusion.5
  294.2 90.2 %all-reduce.3.cloned.1.call-done = (bf16[1024,3,512]{2,0,1:T(8,128)(2,1)}, bf16[512,1024]{1,0:T(8,128)(2,1)}) async-done(((bf16[1024,3,512]{2,0,1:T(8,128)(2,1)}, bf16[512,1024]{1,0:T(8,128)(2,1)}), (bf16[1024,3,512]{2,0,1:T(8,128)(2,1)}, bf16[512,1024]{1,0:T(8,128)(2,1)})) %all-reduce.3.cloned.1.call-update) | async-done | bytes 4194320 | tf_op jit(solution)/shard_map/psum | solution.py:201
  387.3 3.6 convert_element_type.79
  (142 shorter events, 81.0 us)
Async XLA Ops:
  8.0 63.1 %copy-start = (bf16[512,1024]{1,0:T(8,128)(2,1)S(1)}, bf16[512,1024]{1,0:T(8,128)(2,1)}, u32[]{:S(2)}) copy-start(bf16[512,1024]{1,0:T(8,128)(2,1)} %param.11) | copy-start | bytes 3145732
  27.3 4.8 %copy-start.6 = (bf16[1,256,1024]{2,1,0:T(8,128)(2,1)}, bf16[1,256,1024]{2,1,0:T(8,128)(2,1)S(1)}, u32[]{:S(2)}) copy-start(bf16[1,256,1024]{2,1,0:T(8,128)(2,1)S(1)} %all_gather.6) | copy-start | bytes 1572868
  43.6 5.9 %copy-start.11 = (s32[1,4,256]{2,1,0:T(4,128)S(1)}, s32[1,4,256]{2,1,0:T(4,128)}, u32[]{:S(2)}) copy-start(s32[1,4,256]{2,1,0:T(4,128)} %param.12) | copy-start | bytes 12292
  45.1 58.3 %collective-permute-start.2 = (bf16[4,1,192,384]{3,2,0,1:T(8,128)(2,1)}, bf16[4,1,192,384]{3,2,0,1:T(8,128)(2,1)}, u32[]{:S(2)}, u32[]{:S(2)}) collective-permute-start(bf16[4,1,192,384]{3,2,0,1:T(8,128)(2,1)} %get-tuple-element.309), channel_id=1, source_target_pairs={{0,12},{4,8},{8,4},{12,0},{1,13},{5,9},{9,5},{13,1},{2,14},{6,10},... | collective-permute-start | bytes 1769480 | tf_op jit(solution)/shard_map/ppermute | solution.py:33
  48.9 54.5 %collective-permute-start.1 = (bf16[4,1,192,384]{3,2,0,1:T(8,128)(2,1)}, bf16[4,1,192,384]{3,2,0,1:T(8,128)(2,1)}, u32[]{:S(2)}, u32[]{:S(2)}) collective-permute-start(bf16[4,1,192,384]{3,2,0,1:T(8,128)(2,1)} %get-tuple-element.310), channel_id=1, source_target_pairs={{0,8},{4,12},{8,0},{12,4},{1,9},{5,13},{9,1},{13,5},{2,10},{6,14},... | collective-permute-start | bytes 1769480 | tf_op jit(solution)/shard_map/ppermute | solution.py:33
  48.9 54.5 %collective-permute-start = (bf16[4,1,192,384]{3,2,0,1:T(8,128)(2,1)}, bf16[4,1,192,384]{3,2,0,1:T(8,128)(2,1)}, u32[]{:S(2)}, u32[]{:S(2)}) collective-permute-start(bf16[4,1,192,384]{3,2,0,1:T(8,128)(2,1)} %get-tuple-element.311), channel_id=1, source_target_pairs={{0,4},{4,0},{8,12},{12,8},{1,5},{5,1},{9,13},{13,9},{2,6},{6,2},{1... | collective-permute-start | bytes 1769480 | tf_op jit(solution)/shard_map/ppermute | solution.py:33
  57.8 41.1 %all-to-all-start = ((bf16[4,4,192]{2,0,1:T(4,128)(2,1)}), bf16[4,4,192]{2,0,1:T(4,128)(2,1)S(1)}, u32[]{:S(2)}, u32[]{:S(2)}) async-start(bf16[4,4,192]{2,0,1:T(4,128)(2,1)} %copy.68), calls=%async_computation | async-start | bytes 16384 | tf_op jit(solution)/shard_map/all_to_all | solution.py:165
  70.3 0.8 copy-start.1
  98.9 39.4 %all-to-all-start.2 = ((bf16[4,4,192,128]{3,2,0,1:T(8,128)(2,1)}), bf16[4,4,192,128]{3,2,0,1:T(8,128)(2,1)}, u32[]{:S(2)}, u32[]{:S(2)}) async-start(bf16[4,4,192,128]{3,2,0,1:T(8,128)(2,1)} %copy.80), calls=%async_computation.3 | async-start | bytes 1572864 | tf_op jit(solution)/shard_map/all_to_all | solution.py:181
  103.1 3.7 copy-start.10
  138.3 69.1 %all-to-all-start.1 = ((bf16[4,4,192,128]{3,2,0,1:T(8,128)(2,1)}), bf16[4,4,192,128]{3,2,0,1:T(8,128)(2,1)}, u32[]{:S(2)}, u32[]{:S(2)}) async-start(bf16[4,4,192,128]{3,2,0,1:T(8,128)(2,1)} %copy.76), calls=%async_computation.1 | async-start | bytes 1572864 | tf_op jit(solution)/shard_map/all_to_all | solution.py:173
  153.1 3.0 copy-start.9
  171.5 3.0 copy-start.9
  190.4 3.0 copy-start.9
  202.7 1.4 copy-start.8
  207.4 57.5 %all-to-all-start.3 = ((bf16[4,4,192,384]{3,2,0,1:T(8,128)(2,1)}), bf16[4,4,192,384]{3,2,0,1:T(8,128)(2,1)}, u32[]{:S(2)}, u32[]{:S(2)}) async-start(bf16[4,4,192,384]{3,2,0,1:T(8,128)(2,1)} %copy.84), calls=%async_computation.4 | async-start | bytes 4718592 | tf_op jit(solution)/shard_map/all_to_all | solution.py:189
  212.5 171.9 %all-reduce.3.cloned.1.call-start = ((), (), s32[]{:S(2)}) async-start(), calls=%async_computation.8 | async-start | bytes 8388608 | tf_op jit(solution)/shard_map/psum | solution.py:201
  213.7 6.1 %copy-start.2 = (bf16[1,256,1024]{2,1,0:T(8,128)(2,1)S(1)}, bf16[1,256,1024]{2,1,0:T(8,128)(2,1)}, u32[]{:S(2)}) copy-start(bf16[1,256,1024]{2,1,0:T(8,128)(2,1)} %copy-done.1) | copy-start | bytes 1572868
  219.7 1.4 copy-start.4
  279.7 1.1 copy-start.7
  288.1 0.9 copy-start.5
  288.2 102.7 %reduce-scatter.3.cloned.1.call-start = ((), (), s32[]{:S(2)}) async-start(), calls=%async_computation.6 | async-start | bytes 786432 | tf_op jit(solution)/shard_map/reduce_scatter | solution.py:193
  290.4 100.5 %reduce-scatter.5.cloned.1.call-start = ((), (), s32[]{:S(2)}) async-start(), calls=%async_computation.7 | async-start | bytes 786432 | tf_op jit(solution)/shard_map/reduce_scatter | solution.py:205
  384.4 2.9 copy-start.3
Sparse Core Ops, SparseCore 0:
  288.3 96.0 all-reduce.2
Sparse Core Ops, SparseCore 1:
  291.5 13.6 reduce-scatter.2
  307.9 14.5 reduce-scatter.4
